TPU v7x, 256 devices: a whole 4x4x8 slice. The times are simulated.
256 devices in a mesh: pos: 16 (over x, y_hi, core), filt: 8 (over z), layer: 2 (over y_lo).
Axes of the slice: x: 4, y: 4 (y_hi: 2, y_lo: 2; y = y_hi * 2 + y_lo), z: 8, core: 2. Of those that a mesh axis runs over, the one named last changes fastest.
Arguments:
- activations: float32 [512, 1024, 128], P('pos', ('layer', 'filt')), may hold values from -6 to 6
- filters: float32 [9, 1024, 1024], P(None, ('layer', 'pos'), 'filt'), may hold values from -0.0625 to 0.0625
Outputs:
- rectified: float32 [512, 1024, 128], P('pos', ('filt', 'layer'))
All inputs are finite; a program needn't handle non-finite values.
Results may differ from a plain program's by a relative error of at most 0.0001.
Values sent between devices are 32-bit elements; how exact they have to be, the bound alone decides.
A program may use at most 128 MiB of HBM per device.

v0:
```python
import jax
import jax.numpy as jnp
from jax import lax
from jax.sharding import PartitionSpec as P


def extended(block, sides, width):
    for axis, dim in sides:
        count = lax.axis_size(axis)
        forward = [(i, i + 1) for i in range(count - 1)]
        backward = [(target, source) for source, target in forward]
        low = lax.ppermute(
            lax.slice_in_dim(block, block.shape[dim] - width, None, axis=dim), axis, forward
        )
        high = lax.ppermute(lax.slice_in_dim(block, 0, width, axis=dim), axis, backward)
        block = jnp.concatenate([low, block, high], axis=dim)
    return block


def convolve(padded, weights, summed):
    height = padded.shape[0] - 2
    across = padded.shape[2] - 2
    for tap_index in range(9):
        row_shift, col_shift = divmod(tap_index, 3)
        window = padded[row_shift : row_shift + height, :, col_shift : col_shift + across]
        summed = summed + jnp.einsum(
            "ric,io->roc", window, weights[tap_index], precision=lax.Precision.HIGHEST
        )
    return summed


def body(activations, filters):
    panel = lax.all_gather(activations, "filt", axis=1, tiled=True)
    rimmed = extended(panel, (("pos", 0),), 1)
    padded = jnp.pad(rimmed, ((0, 0), (0, 0), (1, 1)))
    height = activations.shape[0]
    across = activations.shape[2]
    empty = jnp.zeros((height, filters.shape[2], across), jnp.float32)
    gathered = lax.all_gather(filters, "pos", axis=1, tiled=True)
    summed = convolve(padded, gathered, empty)
    reduced = lax.psum_scatter(summed, "layer", scatter_dimension=1, tiled=True)
    return jnp.maximum(reduced, 0.0)


def solution(mesh):
    in_specs = (P("pos", ("layer", "filt"), None), P(None, ("layer", "pos"), "filt"))
    out_specs = P("pos", ("filt", "layer"), None)
    return jax.shard_map(body, mesh=mesh, in_specs=in_specs, out_specs=out_specs, check_vma=False)
```

profile of v0, /device:TPU:4, one launch (start us, length us, event | category | flops | bytes accessed | tf_op | source)
XLA Modules:
  0.0 285.2 jit_solution(10424281115399594169)
XLA Ops:
  6.5 0.0 all-gather.3.cloned.1.call-start
  6.5 2.8 copy.6
  9.3 0.0 all-gather.3.cloned.1.call-update
  9.4 0.0 all-gather.5.cloned.1.call-start
  9.4 0.7 all-gather.5.cloned.1.call-update
  10.1 0.0 reduce-scatter.2.cloned.1.call-start
  10.2 96.4 %all-gather.3.cloned.1.call-done = f32[32,512,128]{2,0,1:T(8,128)} async-done(((f32[32,64,128]{2,0,1:T(8,128)}), f32[32,512,128]{2,0,1:T(8,128)}) %all-gather.3.cloned.1.call-update) | async-done | bytes 8388624 | tf_op jit(solution)/shard_map/all_gather | solution.py:33
  106.5 10.0 %copy.7 = f32[32,512,128]{1,2,0:T(8,128)} copy(f32[32,512,128]{2,0,1:T(8,128)} %all-gather.3.cloned.1.call-done) | data formatting | bytes 16777216 | tf_op jit(solution)/shard_map/all_gather | solution.py:33
  116.5 1.1 fusion.26
  117.5 1.9 collective-permute-start
  119.5 6.0 %collective-permute-start.1 = (f32[1,512,128]{1,2,0:T(8,128)S(1)}, f32[1,512,128]{1,2,0:T(8,128)S(1)}, u32[]{:S(2)}, u32[]{:S(2)}) collective-permute-start(f32[1,512,128]{1,2,0:T(8,128)S(1)} %get-tuple-element.6), channel_id=1, source_target_pairs={{16,0},{32,16},{48,32},{64,48},{80,64},{96,80},{112,96},{128,112},... | collective-permute-start | bytes 786440 | tf_op jit(solution)/shard_map/ppermute | solution.py:15
  125.5 35.8 %all-gather.5.cloned.1.call-done = f32[9,512,128]{2,1,0:T(8,128)} async-done(((f32[9,32,128]{2,1,0:T(8,128)}), f32[9,512,128]{2,1,0:T(8,128)}) %all-gather.5.cloned.1.call-update) | async-done | bytes 2359312 | tf_op jit(solution)/shard_map/all_gather | solution.py:39
  161.3 0.0 copy-start
  161.3 9.6 %fusion.23 = f32[32,128,128]{2,1,0:T(8,128)S(1)} fusion(f32[32,512,128]{1,2,0:T(8,128)} %copy.7, f32[9,512,128]{2,1,0:T(8,128)} %all-gather.5.cloned.1.call-done), kind=kOutput, calls=%fused_computation.32 | convolution fusion | flops 3221225472 | bytes 10747904 | tf_op jit(solution)/shard_map/ric,io->roc/dot_general | solution.py:26
  170.9 0.0 collective-permute-done.1
  170.9 0.0 copy-done
  170.9 0.0 copy-done.1
  170.9 7.1 %fusion.5 = f32[32,128,128]{2,1,0:T(8,128)S(1)} fusion(f32[1,512,128]{1,2,0:T(8,128)S(1)} %collective-permute-done.1, f32[32,512,128]{1,2,0:T(8,128)S(1)} %copy-done, f32[9,512,128]{2,1,0:T(8,128)S(1)} %copy-done.1), kind=kOutput, calls=%fused_computation.9 | convolution fusion | flops 3223388160 | bytes 11010048 | tf_op jit(solution)/shard_map/ric,io->roc/dot_general | solution.py:26
  178.1 0.0 collective-permute-done
  178.1 7.5 %fusion.1 = f32[32,128,128]{2,1,0:T(8,128)S(1)} fusion(f32[32,512,128]{1,2,0:T(8,128)S(1)} %copy-done, f32[1,512,128]{1,2,0:T(8,128)S(1)} %collective-permute-done, f32[9,512,128]{2,1,0:T(8,128)S(1)} %copy-done.1), kind=kOutput, calls=%fused_computation.5 | convolution fusion | flops 3223388160 | bytes 11010048 | tf_op jit(solution)/shard_map/ric,io->roc/dot_general | solution.py:26
  185.6 1.9 select_maximum_fusion
  187.5 7.1 %fusion.11 = f32[32,128,128]{2,1,0:T(8,128)S(1)} fusion(f32[34,512,130]{1,2,0:T(8,128)S(1)} %select_maximum_fusion, f32[9,512,128]{2,1,0:T(8,128)S(1)} %copy-done.1), kind=kOutput, calls=%fused_computation.15 | convolution fusion | flops 3221225472 | bytes 10747904 | tf_op jit(solution)/shard_map/ric,io->roc/dot_general | solution.py:26
  194.6 7.2 %fusion.13 = f32[32,128,128]{2,1,0:T(8,128)S(1)} fusion(f32[34,512,130]{1,2,0:T(8,128)S(1)} %select_maximum_fusion, f32[9,512,128]{2,1,0:T(8,128)S(1)} %copy-done.1), kind=kOutput, calls=%fused_computation.17 | convolution fusion | flops 3221225472 | bytes 10747904 | tf_op jit(solution)/shard_map/ric,io->roc/dot_general | solution.py:26
  201.9 8.1 %fusion.15 = f32[32,128,128]{2,1,0:T(8,128)} fusion(f32[34,512,130]{1,2,0:T(8,128)S(1)} %select_maximum_fusion, f32[9,512,128]{2,1,0:T(8,128)S(1)} %copy-done.1), kind=kOutput, calls=%fused_computation.19 | convolution fusion | flops 3221225472 | bytes 10747904 | tf_op jit(solution)/shard_map/ric,io->roc/dot_general | solution.py:26
  210.0 8.3 %fusion.17 = f32[32,128,128]{2,1,0:T(8,128)} fusion(f32[34,512,130]{1,2,0:T(8,128)S(1)} %select_maximum_fusion, f32[9,512,128]{2,1,0:T(8,128)S(1)} %copy-done.1), kind=kOutput, calls=%fused_computation.21 | convolution fusion | flops 3221225472 | bytes 10747904 | tf_op jit(solution)/shard_map/ric,io->roc/dot_general | solution.py:26
  218.3 8.1 %fusion.19 = f32[32,128,128]{2,1,0:T(8,128)} fusion(f32[34,512,130]{1,2,0:T(8,128)S(1)} %select_maximum_fusion, f32[9,512,128]{2,1,0:T(8,128)S(1)} %copy-done.1), kind=kOutput, calls=%fused_computation.23 | convolution fusion | flops 3221225472 | bytes 10747904 | tf_op jit(solution)/shard_map/ric,io->roc/dot_general | solution.py:26
  226.3 9.6 %add_bitcast_fusion = f32[32,128,128]{1,2,0:T(8,128)S(1)} fusion(f32[32,128,128]{2,1,0:T(8,128)S(1)} %fusion.5, f32[32,128,128]{2,1,0:T(8,128)S(1)} %fusion.11, f32[32,128,128]{2,1,0:T(8,128)S(1)} %fusion.13, f32[32,128,128]{2,1,0:T(8,128)S(1)} %fusion.23, f32[32,128,128]{2,1,0:T(8,128)} %fusion.15, f32[32,128,128]{2,1,0:T(8,128)} %fusion.17, ...), kind=kOutput, calls=%fused_computation.25 | convolution fusion | flops 3225419776 | bytes 27525120 | tf_op jit(solution)/shard_map/ric,io->roc/dot_general | solution.py:26
  235.9 2.1 copy.13
  238.0 0.0 reduce-scatter.2.cloned.1.call-update
  238.0 37.5 %reduce-scatter.2.cloned.1.call-done = f32[32,64,128]{2,0,1:T(8,128)} async-done(((f32[32,128,128]{2,0,1:T(8,128)}), f32[32,64,128]{2,0,1:T(8,128)}) %reduce-scatter.2.cloned.1.call-update) | async-done | bytes 1048592 | tf_op jit(solution)/shard_map/reduce_scatter | solution.py:41
  275.5 1.3 broadcast_maximum_fusion
  276.8 1.6 copy.14
  (1 shorter events, 0.0 us)
Async XLA Ops:
  6.5 100.0 %all-gather.3.cloned.1.call-start = ((), (), s32[]{:S(2)}) async-start(), calls=%async_computation.1 | async-start | bytes 9437184 | tf_op jit(solution)/shard_map/all_gather | solution.py:33
  9.4 151.9 %all-gather.5.cloned.1.call-start = ((), (), s32[]{:S(2)}) async-start(), calls=%async_computation.2 | async-start | bytes 2506752 | tf_op jit(solution)/shard_map/all_gather | solution.py:39
  10.1 265.4 %reduce-scatter.2.cloned.1.call-start = ((), (), s32[]{:S(2)}) async-start(), calls=%async_computation.3 | async-start | bytes 3145728 | tf_op jit(solution)/shard_map/reduce_scatter | solution.py:41
  117.5 60.5 %collective-permute-start = (f32[1,512,128]{1,2,0:T(8,128)S(1)}, f32[1,512,128]{1,2,0:T(8,128)S(1)}, u32[]{:S(2)}, u32[]{:S(2)}) collective-permute-start(f32[1,512,128]{1,2,0:T(8,128)S(1)} %get-tuple-element.5), channel_id=1, source_target_pairs={{0,16},{16,32},{32,48},{48,64},{64,80},{80,96},{96,112},{112,128},... | collective-permute-start | bytes 786440 | tf_op jit(solution)/shard_map/ppermute | solution.py:12
  119.5 51.4 %collective-permute-start.1 = (f32[1,512,128]{1,2,0:T(8,128)S(1)}, f32[1,512,128]{1,2,0:T(8,128)S(1)}, u32[]{:S(2)}, u32[]{:S(2)}) collective-permute-start(f32[1,512,128]{1,2,0:T(8,128)S(1)} %get-tuple-element.6), channel_id=1, source_target_pairs={{16,0},{32,16},{48,32},{64,48},{80,64},{96,80},{112,96},{128,112},... | collective-permute-start | bytes 786440 | tf_op jit(solution)/shard_map/ppermute | solution.py:15
  161.3 9.6 %copy-start = (f32[32,512,128]{1,2,0:T(8,128)S(1)}, f32[32,512,128]{1,2,0:T(8,128)}, u32[]{:S(2)}) copy-start(f32[32,512,128]{1,2,0:T(8,128)} %copy.7) | copy-start | bytes 25165828
  161.3 9.6 %copy-start.1 = (f32[9,512,128]{2,1,0:T(8,128)S(1)}, f32[9,512,128]{2,1,0:T(8,128)}, u32[]{:S(2)}) copy-start(f32[9,512,128]{2,1,0:T(8,128)} %all-gather.5.cloned.1.call-done) | copy-start | bytes 7077892
Sparse Core Ops, SparseCore 0:
  9.5 96.9 all-gather.2
  109.3 51.9 all-gather.4
  238.1 37.3 reduce-scatter.1
where the time goes:
time: 290 us; the launch traced here: 285 us
  waiting for transfers between devices  170 us (59%)
  matrix products  72.6 us (25%)
  local copies, waits for them, and re-layouts  17.5 us (6%)
  between operations  13.5 us (5%)
  starting transfers between devices  8.05 us (3%)
  other arithmetic  3.21 us (1%)
    all_gather x1, waiting for transfers between devices, body(): panel = lax.all_gather(activations, 'filt', axis=1, tiled=True)  96.4 us
    dot_general x9, matrix products, convolve(): jnp.einsum('ric,io->roc', window, weights[tap_index], precision=lax.Preci...  72.6 us
    reduce_scatter x1, waiting for transfers between devices, body(): reduced = lax.psum_scatter(summed, 'layer', scatter_dimension=1, tiled=True)  37.5 us
    all_gather x1, waiting for transfers between devices, body(): gathered = lax.all_gather(filters, 'pos', axis=1, tiled=True)  35.8 us
    all_gather x1, local copies, waits for them, and re-layouts, body(): panel = lax.all_gather(activations, 'filt', axis=1, tiled=True)  9.96 us
    ppermute x1, starting transfers between devices, extended(): lax.ppermute(lax.slice_in_dim(block, 0, width, axis=dim), axis, backward)  6.05 us
  transfers between devices with their start and end apart: 5, of which 3 were waited for; matrix products, arithmetic and copies ran while one was open for 10% of the time, Pallas kernels for 0%

commit v1 on v0

v1 whole, which is shorter than its diff:
```python
import jax
import jax.numpy as jnp
from jax import lax
from jax.experimental import pallas as pl
from jax.experimental.pallas import tpu as pltpu
from jax.sharding import PartitionSpec as P

MESH = pl.DeviceIdType.MESH
F32 = jnp.float32
BF16 = jnp.bfloat16
RING = 8
AHEAD = 4


def halves(value):
    high = value.astype(BF16)
    return high, (value - high.astype(F32)).astype(BF16)


def kernel(act, filt, out, ext, taps, xh, xl, wh, wl, part, other,
           loc_sem, halo_send, halo_recv, w_send, w_recv, z_send, z_recv, r_send, r_recv):
    places = lax.axis_size("pos")
    pos, z, layer = lax.axis_index("pos"), lax.axis_index("filt"), lax.axis_index("layer")
    rows, own, cols = act.shape
    depth = filt.shape[1]
    filters = filt.shape[2]
    channels = RING * own
    chunks = (rows + 2) // 2
    chips = places // 2
    core = lax.rem(pos, 2)
    chip = pos // 2
    mate = pos + 1 - 2 * core
    up, down = lax.rem(z + 1, RING), lax.rem(z + RING - 1, RING)
    turn = 1 - 2 * core
    kept = filters // 2

    def remote(src, dst, send, recv, **where):
        return pltpu.make_async_remote_copy(
            src_ref=src, dst_ref=dst, send_sem=send, recv_sem=recv,
            device_id=where, device_id_type=MESH,
        )

    def panel(source, i):
        return ext.at[source, pl.ds(2 * i, 2)]

    def hop(i, slot, source, target):
        block = panel(source, i)
        return remote(block, block, z_send.at[i, slot], z_recv.at[i, slot], filt=target)

    def weights(place):
        return taps.at[:, pl.ds(pl.multiple_of(place * depth, depth), depth)]

    local = pltpu.make_async_copy(act, ext.at[z, pl.ds(1, rows)], loc_sem.at[0])
    local.start()
    local_w = pltpu.make_async_copy(filt, weights(pos), loc_sem.at[1])
    local_w.start()

    @pl.when(pos == 0)
    def _():
        ext[z, 0] = jnp.zeros((own, cols), F32)

    @pl.when(pos == places - 1)
    def _():
        ext[z, rows + 1] = jnp.zeros((own, cols), F32)

    barrier = pltpu.get_barrier_semaphore()
    pl.semaphore_signal(barrier, inc=1, device_id={"filt": up}, device_id_type=MESH)
    pl.semaphore_signal(barrier, inc=1, device_id={"filt": down}, device_id_type=MESH)
    pl.semaphore_signal(barrier, inc=1, device_id={"layer": 1 - layer}, device_id_type=MESH)
    for d in range(1, places):
        pl.semaphore_signal(barrier, inc=1, device_id={"pos": lax.rem(pos + d, places)}, device_id_type=MESH)
    pl.semaphore_wait(barrier, places + 2)

    below = remote(act.at[rows - 1], ext.at[z, 0], halo_send.at[0], halo_recv.at[0], pos=lax.rem(pos + 1, places))
    above = remote(act.at[0], ext.at[z, rows + 1], halo_send.at[1], halo_recv.at[1], pos=lax.rem(pos + places - 1, places))

    @pl.when(pos < places - 1)
    def _():
        below.start()

    @pl.when(pos > 0)
    def _():
        above.start()

    def first(i):
        hop(i, 0, z, up).start()
        hop(i, 1, z, down).start()

    local.wait()
    for i in range(1, AHEAD):
        first(i)
    mine = remote(filt, weights(pos), w_send.at[0], w_recv.at[0], pos=mate)
    mine.start()

    def straight(d):
        target = lax.rem(chip + d, chips) * 2 + core
        return remote(filt, weights(pos), w_send.at[d], w_recv.at[d], pos=target)

    def relay(d):
        block = weights(lax.rem(chip + chips - d, chips) * 2 + core)
        return remote(block, block, w_send.at[chips + d], w_recv.at[chips + d], pos=mate)

    def arrived(d):
        block = weights(lax.rem(chip + chips - d, chips) * 2 + core)
        return remote(block, block, w_send.at[d], w_recv.at[d], pos=mate)

    def relayed(d):
        block = weights(lax.rem(chip + chips - d, chips) * 2 + 1 - core)
        return remote(block, block, w_send.at[chips + d], w_recv.at[chips + d], pos=mate)

    for d in range(1, chips):
        straight(d).start()

    @pl.when(pos > 0)
    def _():
        below.wait_recv()

    first(0)

    def split_rows(r):
        high, low = halves(ext[:, r].reshape(channels, cols))
        xh[r] = high
        xl[r] = low

    def split_taps(t, carry):
        a, b = t // 3, lax.rem(t, 3)
        high, low = halves(taps[t].T)
        at = pl.ds(pl.multiple_of(b * filters, filters), filters)
        wh[a, at] = high
        wl[a, at] = low
        return carry

    lanes = lax.broadcasted_iota(jnp.int32, (filters, cols), 1)

    def swap(k):
        theirs = pl.ds(pl.multiple_of((1 - layer) * kept, kept), kept)
        return remote(part.at[k, :, theirs], other.at[k], r_send.at[k], r_recv.at[k], layer=1 - layer)

    def convolve(k):
        total = None
        for a in range(3):
            high = jnp.concatenate([xh[2 * k + a], xh[2 * k + a + 1]], axis=1)
            low = jnp.concatenate([xl[2 * k + a], xl[2 * k + a + 1]], axis=1)
            for left, right in ((wh, high), (wl, high), (wh, low)):
                term = jnp.dot(left[a], right, preferred_element_type=F32)
                total = term if total is None else total + term
        for q in range(2):
            left, middle, right = [
                total[b * filters : (b + 1) * filters, q * cols : (q + 1) * cols] for b in range(3)
            ]
            left = jnp.where(lanes == 0, 0.0, pltpu.roll(left, 1, 1))
            right = jnp.where(lanes == cols - 1, 0.0, pltpu.roll(right, cols - 1, 1))
            part[k, q] = middle + left + right
        swap(k).start()

    def finish(k):
        swap(k).wait_recv()
        ours = pl.ds(pl.multiple_of(layer * kept, kept), kept)
        out[pl.ds(2 * k, 2)] = part[k, :, ours] + other[k]

    def step(t, carry):
        i = t + AHEAD

        @pl.when(i < chunks)
        def _():
            @pl.when((i == chunks - 1) & (pos < places - 1))
            def _():
                above.wait_recv()

            first(i)

        for h in range(1, 4):
            i = t - (h - 1)

            @pl.when((i >= 0) & (i < chunks))
            def _():
                behind, ahead = lax.rem(z + RING - h, RING), lax.rem(z + h, RING)
                hop(i, 2 * h - 2, behind, up).wait_recv()
                if h < 3:
                    hop(i, 2 * h, behind, up).start()
                hop(i, 2 * h - 1, ahead, down).wait_recv()
                if h < 3:
                    hop(i, 2 * h + 1, ahead, down).start()
                else:
                    hop(i, 6, lax.rem(z + RING - 3 * turn, RING), lax.rem(z + RING + turn, RING)).start()

        for early in range(3):
            @pl.when(t == early)
            def _():
                for d in range(1, chips):
                    if (d - 1) * 3 // (chips - 1) == early:
                        arrived(d).wait_recv()
                        relay(d).start()

        @pl.when(t == 3)
        def _():
            local_w.wait()
            remote(filt, weights(mate), w_send.at[0], w_recv.at[0], pos=mate).wait_recv()
            for d in range(1, chips):
                relayed(d).wait_recv()
            lax.fori_loop(0, 9, split_taps, 0)

        @pl.when(t >= 3)
        def _():
            i = t - 3
            hop(i, 6, lax.rem(z + 4, RING), up).wait_recv()
            split_rows(2 * i)
            split_rows(2 * i + 1)

        @pl.when(t >= 5)
        def _():
            finish(t - 5)

        @pl.when(t >= 4)
        def _():
            convolve(t - 4)

        return carry

    lax.fori_loop(0, chunks + 3, step, 0)
    finish(chunks - 2)

    def drain(i, carry):
        for slot in range(7):
            hop(i, slot, z, up).wait_send()
        return carry

    lax.fori_loop(0, chunks, drain, 0)

    def drain_swap(k, carry):
        swap(k).wait_send()
        return carry

    lax.fori_loop(0, chunks - 1, drain_swap, 0)
    mine.wait_send()
    for d in range(1, chips):
        straight(d).wait_send()
        relay(d).wait_send()

    @pl.when(pos < places - 1)
    def _():
        below.wait_send()

    @pl.when(pos > 0)
    def _():
        above.wait_send()


def body(activations, filters):
    rows, own, cols = activations.shape
    places = lax.axis_size("pos")
    depth, count = filters.shape[1], filters.shape[2]
    channels = RING * own
    chunks = (rows + 2) // 2
    dma = pltpu.SemaphoreType.DMA
    summed = pl.pallas_call(
        kernel,
        out_shape=jax.ShapeDtypeStruct((rows, count // 2, cols), F32),
        in_specs=[pl.BlockSpec(memory_space=pl.ANY)] * 2,
        out_specs=pl.BlockSpec(memory_space=pltpu.VMEM),
        scratch_shapes=[
            pltpu.VMEM((RING, rows + 2, own, cols), F32),
            pltpu.VMEM((9, places * depth, count), F32),
            pltpu.VMEM((rows + 2, channels, cols), BF16),
            pltpu.VMEM((rows + 2, channels, cols), BF16),
            pltpu.VMEM((3, 3 * count, channels), BF16),
            pltpu.VMEM((3, 3 * count, channels), BF16),
            pltpu.VMEM((rows // 2, 2, count, cols), F32),
            pltpu.VMEM((rows // 2, 2, count // 2, cols), F32),
            dma((2,)),
            dma((2,)),
            dma((2,)),
            dma((places,)),
            dma((places,)),
            dma((chunks, 7)),
            dma((chunks, 7)),
            dma((rows // 2,)),
            dma((rows // 2,)),
        ],
        compiler_params=pltpu.CompilerParams(
            collective_id=0, has_side_effects=True, vmem_limit_bytes=48 << 20
        ),
    )(activations, filters)
    return jnp.maximum(summed, 0.0)


def solution(mesh):
    in_specs = (P("pos", ("layer", "filt"), None), P(None, ("layer", "pos"), "filt"))
    out_specs = P("pos", ("filt", "layer"), None)
    return jax.shard_map(body, mesh=mesh, in_specs=in_specs, out_specs=out_specs, check_vma=False)
```

time: 290 us -> 129 us (0.44); the launches traced: 285 us -> 128 us
  waiting for transfers between devices: 170 us -> 0 us
  Pallas kernels: 0 us -> 125 us
  matrix products: 72.6 us -> 0 us
  local copies, waits for them, and re-layouts: 17.5 us -> 2.13 us
  between operations: 13.5 us -> 0.01 us
  starting transfers between devices: 8.05 us -> 0 us
    all_gather x2 -> x0, waiting for transfers between devices: 132 us -> none  [the longest x1 96.4 us: body(): panel = lax.all_gather(activations, 'filt', axis=1, tiled=True)]
    pallas_call x0 -> x1, Pallas kernels: none -> 125 us  [body(): pl.pallas_call(kernel, out_shape=jax.ShapeDtypeStruct((rows, count // 2,...]
    dot_general x9 -> x0, matrix products: 72.6 us -> none  [convolve(): jnp.einsum('ric,io->roc', window, weights[tap_index], precision=lax.Preci...]
    reduce_scatter x1 -> x0, waiting for transfers between devices: 37.5 us -> none  [body(): reduced = lax.psum_scatter(summed, 'layer', scatter_dimension=1, tiled=True)]
    all_gather x1 -> x0, local copies, waits for them, and re-layouts: 9.96 us -> none  [body(): panel = lax.all_gather(activations, 'filt', axis=1, tiled=True)]
    ppermute x2 -> x0, starting transfers between devices: 7.97 us -> none  [the longest x1 6.05 us: extended(): lax.ppermute(lax.slice_in_dim(block, 0, width, axis=dim), axis, backward)]
  transfers between devices with their start and end apart: 5 -> 0, of which waited for: 3 -> 0; matrix products, arithmetic and copies ran while one was open for 10% -> 0% of each run, Pallas kernels for 0% -> 0%
where the time goes in v1:
time: 129 us; the launch traced here: 128 us
  Pallas kernels  125 us (97%)
  local copies, waits for them, and re-layouts  2.13 us (2%)
    pallas_call x1, Pallas kernels, body(): pl.pallas_call(kernel, out_shape=jax.ShapeDtypeStruct((rows, count // 2,...  125 us

profile of v1, /device:TPU:4, one launch (start us, length us, event | category | flops | bytes accessed | tf_op | source)
XLA Modules:
  0.0 128.5 jit_solution(13129694783893590611)
XLA Ops:
  0.0 0.0 copy-start
  0.0 1.2 copy-done
  1.2 0.0 copy-start.1
  1.2 0.9 copy-done.1
  2.1 125.3 %shard_map.28 = f32[32,64,128]{2,1,0:T(8,128)S(1)} custom-call(f32[32,64,128]{2,1,0:T(8,128)S(1)} %copy-done, f32[9,32,128]{2,1,0:T(8,128)S(1)} %copy-done.1), custom_call_target="tpu_custom_call" | custom-call | tf_op jit(solution)/shard_map/pallas_call | solution.py:256
  127.4 1.1 broadcast_maximum_fusion
Async XLA Ops:
  0.0 1.2 copy-start
  1.2 0.9 copy-start.1

commit v2 on v1

v2 whole, which is shorter than its diff:
```python
import jax
import jax.numpy as jnp
from jax import lax
from jax.experimental import pallas as pl
from jax.experimental.pallas import tpu as pltpu
from jax.sharding import PartitionSpec as P

MESH = pl.DeviceIdType.MESH
F32 = jnp.float32
BF16 = jnp.bfloat16
RING = 8
AHEAD = 2
RUN = 4
READY = 3
RELAYS = ((1, (1, 2, 3)), (2, (4, 5, 6, 7)))
EDGES = 7


def halves(value):
    high = value.astype(BF16)
    return high, (value - high.astype(F32)).astype(BF16)


def kernel(act, filt, out, ext, edge, taps, xh, xl, wh, wl, theirs, ours, other,
           loc_sem, halo_send, halo_recv, w_send, w_recv, z_send, z_recv, r_send, r_recv):
    places = lax.axis_size("pos")
    pos, z, layer = lax.axis_index("pos"), lax.axis_index("filt"), lax.axis_index("layer")
    rows, own, cols = act.shape
    depth = filt.shape[1]
    filters = filt.shape[2]
    channels = RING * own
    chunks = rows // RUN
    pairs = rows // 2
    chips = places // 2
    core = lax.rem(pos, 2)
    chip = pos // 2
    mate = pos + 1 - 2 * core
    up, down = lax.rem(z + 1, RING), lax.rem(z + RING - 1, RING)
    turn = 1 - 2 * core
    kept = filters // 2

    def remote(src, dst, send, recv, **where):
        return pltpu.make_async_remote_copy(
            src_ref=src, dst_ref=dst, send_sem=send, recv_sem=recv,
            device_id=where, device_id_type=MESH,
        )

    def panel(source, i):
        return ext.at[source, pl.ds(RUN * i, RUN)]

    def hop(i, slot, source, target):
        block = panel(source, i)
        return remote(block, block, z_send.at[i, slot], z_recv.at[i, slot], filt=target)

    def weights(place):
        return taps.at[:, pl.ds(pl.multiple_of(place * depth, depth), depth)]

    local = [
        pltpu.make_async_copy(act.at[0], ext.at[z, 0], loc_sem.at[0]),
        pltpu.make_async_copy(act.at[rows - 1], ext.at[z, 1], loc_sem.at[2]),
        pltpu.make_async_copy(act.at[pl.ds(1, rows - 2)], ext.at[z, pl.ds(2, rows - 2)], loc_sem.at[3]),
    ]
    for copy in local:
        copy.start()
    local_w = pltpu.make_async_copy(filt, weights(pos), loc_sem.at[1])
    local_w.start()

    @pl.when(pos == 0)
    def _():
        edge[0] = jnp.zeros((RING, own, cols), F32)

    @pl.when(pos == places - 1)
    def _():
        edge[1] = jnp.zeros((RING, own, cols), F32)

    barrier = pltpu.get_barrier_semaphore()
    pl.semaphore_signal(barrier, inc=1, device_id={"filt": up}, device_id_type=MESH)
    pl.semaphore_signal(barrier, inc=1, device_id={"filt": down}, device_id_type=MESH)
    pl.semaphore_signal(barrier, inc=1, device_id={"layer": 1 - layer}, device_id_type=MESH)
    for d in range(1, places):
        pl.semaphore_signal(barrier, inc=1, device_id={"pos": lax.rem(pos + d, places)}, device_id_type=MESH)
    pl.semaphore_wait(barrier, places + 2)

    below = remote(ext.at[:, 1], edge.at[0], halo_send.at[0], halo_recv.at[0], pos=lax.rem(pos + 1, places))
    above = remote(ext.at[:, 0], edge.at[1], halo_send.at[1], halo_recv.at[1], pos=lax.rem(pos + places - 1, places))

    def first(i):
        hop(i, 0, z, up).start()
        hop(i, 1, z, down).start()

    for copy in local:
        copy.wait()
    for i in range(AHEAD):
        first(i)
    mine = remote(filt, weights(pos), w_send.at[0], w_recv.at[0], pos=mate)
    mine.start()

    def straight(d):
        target = lax.rem(chip + d, chips) * 2 + core
        return remote(filt, weights(pos), w_send.at[d], w_recv.at[d], pos=target)

    def relay(d):
        block = weights(lax.rem(chip + chips - d, chips) * 2 + core)
        return remote(block, block, w_send.at[chips + d], w_recv.at[chips + d], pos=mate)

    def arrived(d):
        block = weights(lax.rem(chip + chips - d, chips) * 2 + core)
        return remote(block, block, w_send.at[d], w_recv.at[d], pos=mate)

    def relayed(d):
        block = weights(lax.rem(chip + chips - d, chips) * 2 + 1 - core)
        return remote(block, block, w_send.at[chips + d], w_recv.at[chips + d], pos=mate)

    for d in range(1, chips):
        straight(d).start()

    def split_rows(r, block):
        high, low = halves(block.reshape(channels, cols))
        xh[r] = high
        xl[r] = low

    def split_taps(t, carry):
        a, b = t // 3, lax.rem(t, 3)
        high, low = halves(taps[t].T)
        at = pl.ds(pl.multiple_of(b * kept, kept), kept)
        for owner in range(2):
            side = 1 - owner + layer * (2 * owner - 1)
            taken = slice(owner * kept, (owner + 1) * kept)
            wh[a, side, at] = high[taken]
            wl[a, side, at] = low[taken]
        return carry

    lanes = lax.broadcasted_iota(jnp.int32, (kept, cols), 1)

    def swap(k):
        return remote(theirs.at[k], other.at[k], r_send.at[k], r_recv.at[k], layer=1 - layer)

    def convolve(k, sides):
        first_side, count = sides[0], len(sides)
        height = count * 3 * kept
        total = None
        for a in range(3):
            high = jnp.concatenate([xh[2 * k + a], xh[2 * k + a + 1]], axis=1)
            low = jnp.concatenate([xl[2 * k + a], xl[2 * k + a + 1]], axis=1)
            for left, right in ((wh, high), (wl, high), (wh, low)):
                left = left[a, first_side : first_side + count].reshape(height, channels)
                term = jnp.dot(left, right, preferred_element_type=F32)
                total = term if total is None else total + term
        for n, side in enumerate(sides):
            for q in range(2):
                left, middle, right = [
                    total[(3 * n + b) * kept : (3 * n + b + 1) * kept, q * cols : (q + 1) * cols] for b in range(3)
                ]
                left = jnp.where(lanes == 0, 0.0, pltpu.roll(left, 1, 1))
                right = jnp.where(lanes == cols - 1, 0.0, pltpu.roll(right, cols - 1, 1))
                (theirs, ours)[side][k, q] = middle + left + right

    def whole(k, carry):
        convolve(k, (0, 1))
        swap(k).start()
        return carry

    def finish(k, carry):
        swap(k).wait_recv()
        out[pl.ds(2 * k, 2)] = ours[k] + other[k]
        return carry

    def settle(i):
        hop(i, 6, lax.rem(z + 4, RING), up).wait_recv()

    def split_chunk(i):
        for n in range(RUN):
            split_rows(RUN * i + n, ext[:, RUN * i + n])

    def step(t, carry):
        i = t + AHEAD

        @pl.when(i < chunks)
        def _():
            first(i)

        def through(h):
            i = t - (h - 1)

            @pl.when((i >= 0) & (i < chunks))
            def _():
                behind, ahead = lax.rem(z + RING - h, RING), lax.rem(z + h, RING)
                hop(i, 2 * h - 2, behind, up).wait_recv()
                if h < 3:
                    hop(i, 2 * h, behind, up).start()
                hop(i, 2 * h - 1, ahead, down).wait_recv()
                if h < 3:
                    hop(i, 2 * h + 1, ahead, down).start()
                else:
                    hop(i, 6, lax.rem(z + RING - 3 * turn, RING), lax.rem(z + RING + turn, RING)).start()

        fresh = t >= 5
        k = RUN // 2 * (t - 4) - 1

        through(1)

        @pl.when(fresh)
        def _():
            whole(k, 0)

        through(2)

        @pl.when(fresh)
        def _():
            whole(k + 1, 0)

        through(3)

        for early, group in RELAYS:
            @pl.when(t == early)
            def _():
                for d in group:
                    arrived(d).wait_recv()
                    relay(d).start()

        @pl.when(t == READY)
        def _():
            local_w.wait()
            remote(filt, weights(mate), w_send.at[0], w_recv.at[0], pos=mate).wait_recv()
            for d in range(1, chips):
                relayed(d).wait_recv()
            lax.fori_loop(0, 9, split_taps, 0)

        @pl.when(t == EDGES)
        def _():
            @pl.when(pos > 0)
            def _():
                below.wait_recv()

            @pl.when(pos < places - 1)
            def _():
                above.wait_recv()

            split_rows(0, edge[0])
            split_rows(rows + 1, edge[1])
            whole(0, 0)

        @pl.when(t >= 6)
        def _():
            finish(k - 2, 0)
            finish(k - 1, 0)

        @pl.when(t == 3)
        def _():
            settle(0)

            @pl.when(pos < places - 1)
            def _():
                below.start()

            @pl.when(pos > 0)
            def _():
                above.start()

            split_rows(1, ext[:, 0])
            split_rows(rows, ext[:, 1])
            split_rows(2, ext[:, 2])
            split_rows(3, ext[:, 3])

        @pl.when(t > 3)
        def _():
            settle(t - 3)
            split_chunk(t - 3)

        return carry

    lax.fori_loop(0, chunks + 3, step, 0)
    late = pairs - 3
    lax.fori_loop(late, pairs, lambda k, carry: (convolve(k, (0,)), swap(k).start(), carry)[2], 0)
    finish(0, 0)
    finish(late - 2, 0)
    finish(late - 1, 0)
    lax.fori_loop(late, pairs, lambda k, carry: (convolve(k, (1,)), carry)[1], 0)
    lax.fori_loop(late, pairs, finish, 0)

    def drain(i, carry):
        for slot in range(7):
            hop(i, slot, z, up).wait_send()
        return carry

    lax.fori_loop(0, chunks, drain, 0)

    def drain_swap(k, carry):
        swap(k).wait_send()
        return carry

    lax.fori_loop(0, pairs, drain_swap, 0)
    mine.wait_send()
    for d in range(1, chips):
        straight(d).wait_send()
        relay(d).wait_send()

    @pl.when(pos < places - 1)
    def _():
        below.wait_send()

    @pl.when(pos > 0)
    def _():
        above.wait_send()


def body(activations, filters):
    rows, own, cols = activations.shape
    places = lax.axis_size("pos")
    depth, count = filters.shape[1], filters.shape[2]
    channels = RING * own
    chunks = rows // RUN
    dma = pltpu.SemaphoreType.DMA
    summed = pl.pallas_call(
        kernel,
        out_shape=jax.ShapeDtypeStruct((rows, count // 2, cols), F32),
        in_specs=[pl.BlockSpec(memory_space=pl.ANY)] * 2,
        out_specs=pl.BlockSpec(memory_space=pltpu.VMEM),
        scratch_shapes=[
            pltpu.VMEM((RING, rows, own, cols), F32),
            pltpu.VMEM((2, RING, own, cols), F32),
            pltpu.VMEM((9, places * depth, count), F32),
            pltpu.VMEM((rows + 2, channels, cols), BF16),
            pltpu.VMEM((rows + 2, channels, cols), BF16),
            pltpu.VMEM((3, 2, 3 * count // 2, channels), BF16),
            pltpu.VMEM((3, 2, 3 * count // 2, channels), BF16),
            pltpu.VMEM((rows // 2, 2, count // 2, cols), F32),
            pltpu.VMEM((rows // 2, 2, count // 2, cols), F32),
            pltpu.VMEM((rows // 2, 2, count // 2, cols), F32),
            dma((4,)),
            dma((2,)),
            dma((2,)),
            dma((places,)),
            dma((places,)),
            dma((chunks, 7)),
            dma((chunks, 7)),
            dma((rows // 2,)),
            dma((rows // 2,)),
        ],
        compiler_params=pltpu.CompilerParams(
            collective_id=0, has_side_effects=True, vmem_limit_bytes=67043328
        ),
    )(activations, filters)
    return jnp.maximum(summed, 0.0)


def solution(mesh):
    in_specs = (P("pos", ("layer", "filt"), None), P(None, ("layer", "pos"), "filt"))
    out_specs = P("pos", ("filt", "layer"), None)
    return jax.shard_map(body, mesh=mesh, in_specs=in_specs, out_specs=out_specs, check_vma=False)
```

time: 129 us -> 104 us (0.81)
  Pallas kernels: 125 us -> 100 us
  local copies, waits for them, and re-layouts: 2.13 us -> 0 us
    pallas_call x1, Pallas kernels: 125 us -> 100 us  [body(): pl.pallas_call(kernel, out_shape=jax.ShapeDtypeStruct((rows, count // 2,...]
    unnamed x4 -> x0, local copies, waits for them, and re-layouts: 2.13 us -> none
where the time goes in v2:
time: 104 us; the launch traced here: 103 us
  Pallas kernels  100 us (96%)
  other arithmetic  2.31 us (2%)
    pallas_call x1, Pallas kernels, body(): pl.pallas_call(kernel, out_shape=jax.ShapeDtypeStruct((rows, count // 2,...  100 us
    max x1, other arithmetic, body(): return jnp.maximum(summed, 0.0)  2.31 us

profile of v2, /device:TPU:4, one launch (start us, length us, event | category | flops | bytes accessed | tf_op | source)
XLA Modules:
  0.0 102.5 jit_solution(4567154951648970307)
XLA Ops:
  0.0 100.2 %shard_map.28 = f32[32,64,128]{2,1,0:T(8,128)} custom-call(f32[32,64,128]{2,1,0:T(8,128)} %act.1, f32[9,32,128]{2,1,0:T(8,128)} %filt.1), custom_call_target="tpu_custom_call" | custom-call | tf_op jit(solution)/shard_map/pallas_call | solution.py:314
  100.2 2.3 %broadcast_maximum_fusion = f32[32,64,128]{2,1,0:T(8,128)} fusion(f32[32,64,128]{2,1,0:T(8,128)} %shard_map.28), kind=kLoop, calls=%fused_computation | loop fusion | flops 262144 | bytes 2097152 | tf_op jit(solution)/shard_map/max | solution.py:344

commit v3 on v2

--- a/solution.py
+++ b/solution.py
@@ -12,7 +12,8 @@
 AHEAD = 2
 RUN = 4
 READY = 3
-RELAYS = ((1, (1, 2, 3)), (2, (4, 5, 6, 7)))
+RELAYS = ((0, (1, 2, 3)), (1, (4, 5, 6)), (2, (7,)))
+SHARDS = {1: (0, 1), 2: (-1, 0), 3: (1, 0), 4: (-1, 1), 5: (1, 1), 6: (-2, 0), 7: (2, 1)}
 EDGES = 7
 
 
@@ -31,9 +32,11 @@
     channels = RING * own
     chunks = rows // RUN
     pairs = rows // 2
-    chips = places // 2
+    across = places // 4
     core = lax.rem(pos, 2)
-    chip = pos // 2
+    half = lax.rem(pos // 2, 2)
+    facing = pos + 2 - 4 * half
+    after, before = lax.rem(pos + 4, places), lax.rem(pos + places - 4, places)
     mate = pos + 1 - 2 * core
     up, down = lax.rem(z + 1, RING), lax.rem(z + RING - 1, RING)
     turn = 1 - 2 * core
@@ -77,9 +80,10 @@
     pl.semaphore_signal(barrier, inc=1, device_id={"filt": up}, device_id_type=MESH)
     pl.semaphore_signal(barrier, inc=1, device_id={"filt": down}, device_id_type=MESH)
     pl.semaphore_signal(barrier, inc=1, device_id={"layer": 1 - layer}, device_id_type=MESH)
-    for d in range(1, places):
-        pl.semaphore_signal(barrier, inc=1, device_id={"pos": lax.rem(pos + d, places)}, device_id_type=MESH)
-    pl.semaphore_wait(barrier, places + 2)
+    near = (lax.rem(pos + 1, places), lax.rem(pos + places - 1, places), after, before, facing)
+    for place in near:
+        pl.semaphore_signal(barrier, inc=1, device_id={"pos": place}, device_id_type=MESH)
+    pl.semaphore_wait(barrier, len(near) + 3)
 
     below = remote(ext.at[:, 1], edge.at[0], halo_send.at[0], halo_recv.at[0], pos=lax.rem(pos + 1, places))
     above = remote(ext.at[:, 0], edge.at[1], halo_send.at[1], halo_recv.at[1], pos=lax.rem(pos + places - 1, places))
@@ -92,27 +96,37 @@
         copy.wait()
     for i in range(AHEAD):
         first(i)
-    mine = remote(filt, weights(pos), w_send.at[0], w_recv.at[0], pos=mate)
-    mine.start()
-
-    def straight(d):
-        target = lax.rem(chip + d, chips) * 2 + core
-        return remote(filt, weights(pos), w_send.at[d], w_recv.at[d], pos=target)
-
-    def relay(d):
-        block = weights(lax.rem(chip + chips - d, chips) * 2 + core)
-        return remote(block, block, w_send.at[chips + d], w_recv.at[chips + d], pos=mate)
-
-    def arrived(d):
-        block = weights(lax.rem(chip + chips - d, chips) * 2 + core)
-        return remote(block, block, w_send.at[d], w_recv.at[d], pos=mate)
-
-    def relayed(d):
-        block = weights(lax.rem(chip + chips - d, chips) * 2 + 1 - core)
-        return remote(block, block, w_send.at[chips + d], w_recv.at[chips + d], pos=mate)
-
-    for d in range(1, chips):
-        straight(d).start()
+    def shard(n, side):
+        dx, flip = SHARDS[n]
+        row = lax.rem(pos // 4 + across + dx, across)
+        return weights(4 * row + 2 * (1 - half if flip else half) + side)
+
+    own_sends = [
+        remote(filt, weights(pos), w_send.at[0], w_recv.at[0], pos=mate),
+        remote(filt, weights(pos), w_send.at[1], w_recv.at[1], pos=facing),
+        remote(filt, weights(pos), w_send.at[2], w_recv.at[2], pos=after),
+        remote(filt, weights(pos), w_send.at[3], w_recv.at[3], pos=before),
+    ]
+    onward = ((1, 4, after), (1, 5, before), (2, 6, after), (5, 7, before))
+
+    def relays(n):
+        block = shard(n, core)
+        sends = [remote(block, block, w_send.at[3 + n], w_recv.at[8 + n], pos=mate)]
+        for source, arrival, target in onward:
+            if source == n:
+                sends.append(remote(block, block, w_send.at[7 + arrival], w_recv.at[arrival], pos=target))
+        return sends
+
+    def arrived(n):
+        block = shard(n, core)
+        return remote(block, block, w_send.at[0], w_recv.at[n], pos=mate)
+
+    def relayed(n):
+        block = shard(n, 1 - core)
+        return remote(block, block, w_send.at[0], w_recv.at[8 + n], pos=mate)
+
+    for send in own_sends:
+        send.start()
 
     def split_rows(r, block):
         high, low = halves(block.reshape(channels, cols))
@@ -216,13 +230,14 @@
             def _():
                 for d in group:
                     arrived(d).wait_recv()
-                    relay(d).start()
+                    for send in relays(d):
+                        send.start()
 
         @pl.when(t == READY)
         def _():
             local_w.wait()
             remote(filt, weights(mate), w_send.at[0], w_recv.at[0], pos=mate).wait_recv()
-            for d in range(1, chips):
+            for d in SHARDS:
                 relayed(d).wait_recv()
             lax.fori_loop(0, 9, split_taps, 0)
 
@@ -290,10 +305,11 @@
         return carry
 
     lax.fori_loop(0, pairs, drain_swap, 0)
-    mine.wait_send()
-    for d in range(1, chips):
-        straight(d).wait_send()
-        relay(d).wait_send()
+    for send in own_sends:
+        send.wait_send()
+    for d in SHARDS:
+        for send in relays(d):
+            send.wait_send()
 
     @pl.when(pos < places - 1)
     def _():
@@ -314,7 +330,7 @@
     summed = pl.pallas_call(
         kernel,
         out_shape=jax.ShapeDtypeStruct((rows, count // 2, cols), F32),
-        in_specs=[pl.BlockSpec(memory_space=pl.ANY)] * 2,
+        in_specs=[pl.BlockSpec(memory_space=pltpu.HBM)] * 2,
         out_specs=pl.BlockSpec(memory_space=pltpu.VMEM),
         scratch_shapes=[
             pltpu.VMEM((RING, rows, own, cols), F32),
@@ -338,9 +354,9 @@
             dma((rows // 2,)),
         ],
         compiler_params=pltpu.CompilerParams(
-            collective_id=0, has_side_effects=True, vmem_limit_bytes=67043328
+            collective_id=0, has_side_effects=True, vmem_limit_bytes=34 << 20
         ),
-    )(activations, filters)
+    )(pltpu.with_memory_space_constraint(activations, pltpu.HBM), pltpu.with_memory_space_constraint(filters, pltpu.HBM))
     return jnp.maximum(summed, 0.0)
 
 

time: 104 us -> 100 us (0.962); the launches traced: 103 us -> 100 us
  other arithmetic: 2.31 us -> 1.09 us
    max x1, other arithmetic: 2.31 us -> 1.09 us  [body(): return jnp.maximum(summed, 0.0)]
    pallas_call x1, Pallas kernels: 100 us -> 99 us  [body(): pl.pallas_call(kernel, out_shape=jax.ShapeDtypeStruct((rows, count // 2,...]
where the time goes in v3:
time: 100 us
  Pallas kernels  99 us (99%)
  other arithmetic  1.09 us (1%)
    pallas_call x1, Pallas kernels, body(): pl.pallas_call(kernel, out_shape=jax.ShapeDtypeStruct((rows, count // 2,...  99 us

profile of v3, /device:TPU:4, one launch (start us, length us, event | category | flops | bytes accessed | tf_op | source)
XLA Modules:
  0.0 100.1 jit_solution(12957125723329747950)
XLA Ops:
  0.0 99.0 %shard_map.28 = f32[32,64,128]{2,1,0:T(8,128)S(1)} custom-call(f32[32,64,128]{2,1,0:T(8,128)} %act.1, f32[9,32,128]{2,1,0:T(8,128)} %filt.1), custom_call_target="tpu_custom_call" | custom-call | tf_op jit(solution)/shard_map/pallas_call | solution.py:330
  99.0 1.1 %broadcast_maximum_fusion = f32[32,64,128]{2,1,0:T(8,128)} fusion(f32[32,64,128]{2,1,0:T(8,128)S(1)} %shard_map.28), kind=kLoop, calls=%fused_computation | loop fusion | flops 262144 | bytes 2097152 | tf_op jit(solution)/shard_map/max | solution.py:360

commit v4 on v3

--- a/solution.py
+++ b/solution.py
@@ -88,6 +88,11 @@
     below = remote(ext.at[:, 1], edge.at[0], halo_send.at[0], halo_recv.at[0], pos=lax.rem(pos + 1, places))
     above = remote(ext.at[:, 0], edge.at[1], halo_send.at[1], halo_recv.at[1], pos=lax.rem(pos + places - 1, places))
 
+    def part(n, source, target):
+        block = ext.at[source, pl.ds(RUN * (chunks - 1) + 2 * n, 2)]
+        at = chunks - 1 + n
+        return remote(block, block, z_send.at[at, 6], z_recv.at[at, 6], filt=target)
+
     def first(i):
         hop(i, 0, z, up).start()
         hop(i, 1, z, down).start()
@@ -206,22 +211,31 @@
                 if h < 3:
                     hop(i, 2 * h + 1, ahead, down).start()
                 else:
-                    hop(i, 6, lax.rem(z + RING - 3 * turn, RING), lax.rem(z + RING + turn, RING)).start()
+                    source, target = lax.rem(z + RING - 3 * turn, RING), lax.rem(z + RING + turn, RING)
+
+                    @pl.when(i < chunks - 1)
+                    def _():
+                        hop(i, 6, source, target).start()
+
+                    @pl.when(i == chunks - 1)
+                    def _():
+                        for n in range(2):
+                            part(n, source, target).start()
 
         fresh = t >= 5
         k = RUN // 2 * (t - 4) - 1
 
+        @pl.when(fresh)
+        def _():
+            whole(k, 0)
+
         through(1)
 
         @pl.when(fresh)
         def _():
-            whole(k, 0)
+            whole(k + 1, 0)
 
         through(2)
-
-        @pl.when(fresh)
-        def _():
-            whole(k + 1, 0)
 
         through(3)
 
@@ -277,7 +291,7 @@
             split_rows(2, ext[:, 2])
             split_rows(3, ext[:, 3])
 
-        @pl.when(t > 3)
+        @pl.when((t > 3) & (t < chunks + 2))
         def _():
             settle(t - 3)
             split_chunk(t - 3)
@@ -285,20 +299,33 @@
         return carry
 
     lax.fori_loop(0, chunks + 3, step, 0)
-    late = pairs - 3
+    for n in range(2):
+        part(n, lax.rem(z + 4, RING), up).wait_recv()
+        for at in (rows - 4 + 2 * n, rows - 3 + 2 * n):
+            split_rows(at, ext[:, at])
+        if n == 0:
+            convolve(pairs - 3, (0,))
+            swap(pairs - 3).start()
+    late = pairs - 2
     lax.fori_loop(late, pairs, lambda k, carry: (convolve(k, (0,)), swap(k).start(), carry)[2], 0)
+    lax.fori_loop(late - 1, pairs, lambda k, carry: (convolve(k, (1,)), carry)[1], 0)
     finish(0, 0)
-    finish(late - 2, 0)
-    finish(late - 1, 0)
-    lax.fori_loop(late, pairs, lambda k, carry: (convolve(k, (1,)), carry)[1], 0)
-    lax.fori_loop(late, pairs, finish, 0)
+    lax.fori_loop(late - 3, pairs, finish, 0)
 
     def drain(i, carry):
-        for slot in range(7):
+        for slot in range(6):
             hop(i, slot, z, up).wait_send()
+
+        @pl.when(i < chunks - 1)
+        def _():
+            hop(i, 6, z, up).wait_send()
+
         return carry
 
     lax.fori_loop(0, chunks, drain, 0)
+
+    for n in range(2):
+        part(n, z, up).wait_send()
 
     def drain_swap(k, carry):
         swap(k).wait_send()
@@ -348,8 +375,8 @@
             dma((2,)),
             dma((places,)),
             dma((places,)),
-            dma((chunks, 7)),
-            dma((chunks, 7)),
+            dma((chunks + 1, 7)),
+            dma((chunks + 1, 7)),
             dma((rows // 2,)),
             dma((rows // 2,)),
         ],

time: 100 us -> 99.5 us (level)
  no operation moved by 1% of the time
where the time goes in v4:
time: 99.5 us; the launch traced here: 99.4 us
  Pallas kernels  98.3 us (99%)
  other arithmetic  1.09 us (1%)
    pallas_call x1, Pallas kernels, body(): pl.pallas_call(kernel, out_shape=jax.ShapeDtypeStruct((rows, count // 2,...  98.3 us

profile of v4, /device:TPU:4, one launch (start us, length us, event | category | flops | bytes accessed | tf_op | source)
XLA Modules:
  0.0 99.4 jit_solution(3440976074861738469)
XLA Ops:
  0.0 98.3 %shard_map.28 = f32[32,64,128]{2,1,0:T(8,128)S(1)} custom-call(f32[32,64,128]{2,1,0:T(8,128)} %act.1, f32[9,32,128]{2,1,0:T(8,128)} %filt.1), custom_call_target="tpu_custom_call" | custom-call | tf_op jit(solution)/shard_map/pallas_call | solution.py:357
  98.3 1.1 %broadcast_maximum_fusion = f32[32,64,128]{2,1,0:T(8,128)} fusion(f32[32,64,128]{2,1,0:T(8,128)S(1)} %shard_map.28), kind=kLoop, calls=%fused_computation | loop fusion | flops 262144 | bytes 2097152 | tf_op jit(solution)/shard_map/max | solution.py:387

commit v5 on v4

--- a/solution.py
+++ b/solution.py
@@ -94,8 +94,8 @@
         return remote(block, block, z_send.at[at, 6], z_recv.at[at, 6], filt=target)
 
     def first(i):
-        hop(i, 0, z, up).start()
-        hop(i, 1, z, down).start()
+        hop(i, core, z, lax.rem(z + RING + turn, RING)).start()
+        hop(i, 1 - core, z, lax.rem(z + RING - turn, RING)).start()
 
     for copy in local:
         copy.wait()
@@ -203,13 +203,11 @@
 
             @pl.when((i >= 0) & (i < chunks))
             def _():
-                behind, ahead = lax.rem(z + RING - h, RING), lax.rem(z + h, RING)
-                hop(i, 2 * h - 2, behind, up).wait_recv()
+                hop(i, 2 * h - 2 + core, lax.rem(z + RING - h * turn, RING), up).wait_recv()
                 if h < 3:
-                    hop(i, 2 * h, behind, up).start()
-                hop(i, 2 * h - 1, ahead, down).wait_recv()
-                if h < 3:
-                    hop(i, 2 * h + 1, ahead, down).start()
+                    hop(i, 2 * h + core, lax.rem(z + RING - h * turn, RING), lax.rem(z + RING + turn, RING)).start()
+                    hop(i, 2 * h - 1 - core, lax.rem(z + RING + h * turn, RING), up).wait_recv()
+                    hop(i, 2 * h + 1 - core, lax.rem(z + RING + h * turn, RING), lax.rem(z + RING - turn, RING)).start()
                 else:
                     source, target = lax.rem(z + RING - 3 * turn, RING), lax.rem(z + RING + turn, RING)
 
@@ -222,8 +220,24 @@
                         for n in range(2):
                             part(n, source, target).start()
 
+                    hop(i, 2 * h - 1 - core, lax.rem(z + RING + h * turn, RING), up).wait_recv()
+
         fresh = t >= 5
         k = RUN // 2 * (t - 4) - 1
+
+        @pl.when(t == EDGES)
+        def _():
+            @pl.when(pos > 0)
+            def _():
+                below.wait_recv()
+
+            @pl.when(pos < places - 1)
+            def _():
+                above.wait_recv()
+
+            split_rows(0, edge[0])
+            split_rows(rows + 1, edge[1])
+            whole(0, 0)
 
         @pl.when(fresh)
         def _():
@@ -255,25 +269,6 @@
                 relayed(d).wait_recv()
             lax.fori_loop(0, 9, split_taps, 0)
 
-        @pl.when(t == EDGES)
-        def _():
-            @pl.when(pos > 0)
-            def _():
-                below.wait_recv()
-
-            @pl.when(pos < places - 1)
-            def _():
-                above.wait_recv()
-
-            split_rows(0, edge[0])
-            split_rows(rows + 1, edge[1])
-            whole(0, 0)
-
-        @pl.when(t >= 6)
-        def _():
-            finish(k - 2, 0)
-            finish(k - 1, 0)
-
         @pl.when(t == 3)
         def _():
             settle(0)
@@ -295,6 +290,11 @@
         def _():
             settle(t - 3)
             split_chunk(t - 3)
+
+        @pl.when(t >= 6)
+        def _():
+            finish(k - 2, 0)
+            finish(k - 1, 0)
 
         return carry
 

time: 99.5 us -> 99.8 us (level)
  no operation moved by 1% of the time
where the time goes in v5:
time: 99.8 us; the launch traced here: 99.7 us
  Pallas kernels  98.6 us (99%)
  other arithmetic  1.09 us (1%)
    pallas_call x1, Pallas kernels, body(): pl.pallas_call(kernel, out_shape=jax.ShapeDtypeStruct((rows, count // 2,...  98.6 us

profile of v5, /device:TPU:4, one launch (start us, length us, event | category | flops | bytes accessed | tf_op | source)
XLA Modules:
  0.0 99.7 jit_solution(4167103492108185657)
XLA Ops:
  0.0 98.6 %shard_map.28 = f32[32,64,128]{2,1,0:T(8,128)S(1)} custom-call(f32[32,64,128]{2,1,0:T(8,128)} %act.1, f32[9,32,128]{2,1,0:T(8,128)} %filt.1), custom_call_target="tpu_custom_call" | custom-call | tf_op jit(solution)/shard_map/pallas_call | solution.py:357
  98.6 1.1 %broadcast_maximum_fusion = f32[32,64,128]{2,1,0:T(8,128)} fusion(f32[32,64,128]{2,1,0:T(8,128)S(1)} %shard_map.28), kind=kLoop, calls=%fused_computation | loop fusion | flops 262144 | bytes 2097152 | tf_op jit(solution)/shard_map/max | solution.py:387

commit v6 on v4

--- a/solution.py
+++ b/solution.py
@@ -225,6 +225,20 @@
         fresh = t >= 5
         k = RUN // 2 * (t - 4) - 1
 
+        @pl.when(t == EDGES)
+        def _():
+            @pl.when(pos > 0)
+            def _():
+                below.wait_recv()
+
+            @pl.when(pos < places - 1)
+            def _():
+                above.wait_recv()
+
+            split_rows(0, edge[0])
+            split_rows(rows + 1, edge[1])
+            whole(0, 0)
+
         @pl.when(fresh)
         def _():
             whole(k, 0)
@@ -254,20 +268,6 @@
             for d in SHARDS:
                 relayed(d).wait_recv()
             lax.fori_loop(0, 9, split_taps, 0)
-
-        @pl.when(t == EDGES)
-        def _():
-            @pl.when(pos > 0)
-            def _():
-                below.wait_recv()
-
-            @pl.when(pos < places - 1)
-            def _():
-                above.wait_recv()
-
-            split_rows(0, edge[0])
-            split_rows(rows + 1, edge[1])
-            whole(0, 0)
 
         @pl.when(t >= 6)
         def _():

time: 99.5 us -> 99.6 us (level)
  no operation moved by 1% of the time
where the time goes in v6:
time: 99.6 us; the launch traced here: 99.5 us
  Pallas kernels  98.4 us (99%)
  other arithmetic  1.09 us (1%)
    pallas_call x1, Pallas kernels, body(): pl.pallas_call(kernel, out_shape=jax.ShapeDtypeStruct((rows, count // 2,...  98.4 us

profile of v6, /device:TPU:4, one launch (start us, length us, event | category | flops | bytes accessed | tf_op | source)
XLA Modules:
  0.0 99.5 jit_solution(16000373890463116246)
XLA Ops:
  0.0 98.4 %shard_map.28 = f32[32,64,128]{2,1,0:T(8,128)S(1)} custom-call(f32[32,64,128]{2,1,0:T(8,128)} %act.1, f32[9,32,128]{2,1,0:T(8,128)} %filt.1), custom_call_target="tpu_custom_call" | custom-call | tf_op jit(solution)/shard_map/pallas_call | solution.py:357
  98.4 1.1 %broadcast_maximum_fusion = f32[32,64,128]{2,1,0:T(8,128)} fusion(f32[32,64,128]{2,1,0:T(8,128)S(1)} %shard_map.28), kind=kLoop, calls=%fused_computation | loop fusion | flops 262144 | bytes 2097152 | tf_op jit(solution)/shard_map/max | solution.py:387
